TPU v7x, 256 devices: a whole 4x4x8 slice. The times are simulated.
256 devices in a mesh: row: 8 (over z), col: 32 (over y, x, core).
Axes of the slice: x: 4, y: 4, z: 8, core: 2. Of those that a mesh axis runs over, the one named last changes fastest.
Arguments:
- factor: bfloat16 [32, 8, 8, 32, 128, 128], P(None, 'row', None, 'col'), may hold values from -0.046875 to 0.046875
- pattern: int32 [32, 8, 8, 32], P(None, 'row', None, 'col'), may hold values 0 or 1
- loads: float32 [8, 32, 128, 256], P(None, 'col'), may hold values from -6 to 6
- block_inverse: float32 [8, 32, 128, 128], P(None, 'col'), may hold values from -1 to 2, as said below
Outputs:
- solution: float32 [8, 32, 128, 256], P(None, 'col')
Inputs may be any that keep to these rules, and one draw needn't show every extreme that they name: `block_inverse`: each block is lower triangular with diagonal entries between 0.5 and 1.5.
All inputs are finite; a program needn't handle non-finite values. No bound on the sum of `pattern` on one device may be relied on, other than what follows from the above.
Results may differ from a plain program's by a relative error of at most 0.0045.
Values may be sent and summed in bfloat16 or wider, within the bound.
No kernel may reach another device: no remote copies, remote signals or barrier semaphores. Data moves between devices by JAX's collectives and lax.ppermute only.
A program may use at most 128 MiB of HBM per device.

v0:
```python
import jax
import jax.numpy as jnp
from jax import lax
from jax.sharding import PartitionSpec as P

LEVELS = 8


def spread(value, axis, source):
    kept = jnp.where(lax.axis_index(axis) == source, value, 0).astype(value.dtype)
    return lax.psum(kept, axis)


def per_device(factor, pattern, loads, block_inverse):
    row_count = lax.axis_size("row")
    col_count = lax.axis_size("col")
    groups = col_count // row_count
    my_row = lax.axis_index("row")
    my_col = lax.axis_index("col")
    masked = factor[:, 0, :, 0] * pattern[:, 0, :, 0].astype(jnp.bfloat16)[:, :, None, None]
    per_row = factor.shape[0] // LEVELS
    per_col = factor.shape[2] // LEVELS
    rhs_local = loads[:, 0]
    inverse_local = block_inverse[:, 0]
    forward_vals = []
    forward_low = []
    for level_id in range(LEVELS):
        rhs_level = rhs_local[level_id * per_col : (level_id + 1) * per_col]
        inverse_level = inverse_local[level_id * per_col : (level_id + 1) * per_col]
        if level_id > 0:
            panel = masked[level_id * per_row : (level_id + 1) * per_row, : level_id * per_col]
            earlier = jnp.concatenate(forward_low, axis=0)
            partial_sum = jnp.einsum(
                "abpq,bqs->aps", panel, earlier, preferred_element_type=jnp.float32
            )
            row_total = lax.psum(partial_sum, "col")
            row_total = row_total.reshape((per_col, groups) + row_total.shape[1:])
            own_total = lax.dynamic_index_in_dim(
                row_total, my_col // row_count, axis=1, keepdims=False
            )
            solved = jnp.einsum(
                "mpq,mqs->mps",
                inverse_level,
                rhs_level - own_total,
                precision=lax.Precision.HIGHEST,
            )
            solved = spread(solved, "row", my_col % row_count)
        else:
            solved = jnp.einsum(
                "mpq,mqs->mps", inverse_level, rhs_level, precision=lax.Precision.HIGHEST
            )
        forward_vals.append(solved)
        forward_low.append(solved.astype(jnp.bfloat16))
    solution_parts = [None] * LEVELS
    later = []
    for level_id in reversed(range(LEVELS)):
        inverse_level = inverse_local[level_id * per_col : (level_id + 1) * per_col]
        resid = forward_vals[level_id]
        if level_id < LEVELS - 1:
            panel = masked[
                (level_id + 1) * per_row :, level_id * per_col : (level_id + 1) * per_col
            ]
            after = jnp.concatenate(later, axis=0)
            partial_sum = jnp.einsum(
                "abpq,aps->bqs", panel, after, preferred_element_type=jnp.float32
            )
            resid = resid - lax.psum(partial_sum, "row")
        solved = jnp.einsum("mqp,mqs->mps", inverse_level, resid, precision=lax.Precision.HIGHEST)
        solution_parts[level_id] = solved
        if level_id > 0:
            low_solved = solved.astype(jnp.bfloat16)
            pieces = lax.all_gather(low_solved[None], "col", axis=0, tiled=True)
            pieces = pieces.reshape((groups, row_count) + low_solved.shape)
            picked = lax.dynamic_index_in_dim(pieces, my_row, axis=1, keepdims=False)
            arranged = jnp.swapaxes(picked, 0, 1).reshape((per_row,) + low_solved.shape[1:])
            later = [arranged] + later
    solution = jnp.concatenate(solution_parts, axis=0)
    return solution[:, None]


def solution(mesh):
    in_specs = (
        P(None, "row", None, "col", None, None),
        P(None, "row", None, "col"),
        P(None, "col", None, None),
        P(None, "col", None, None),
    )
    out_specs = P(None, "col", None, None)
    return jax.shard_map(
        per_device, mesh=mesh, in_specs=in_specs, out_specs=out_specs, check_vma=False
    )
```

profile of v0, /device:TPU:2, one launch (start us, length us, event | category | flops | bytes accessed | tf_op | source)
XLA Modules:
  0.0 2246.1 jit_solution(3896068341786399089)
XLA Ops:
  8.5 7.4 bitcast_multiply_fusion
  17.9 116.1 %all-reduce.22.cloned.1.call-done = f32[4,128,256]{2,1,0:T(8,128)} async-done(((f32[4,128,256]{2,1,0:T(8,128)}), f32[4,128,256]{2,1,0:T(8,128)}) %all-reduce.22.cloned.1.call-update) | async-done | bytes 524304 | tf_op jit(solution)/shard_map/psum | solution.py:36
  135.9 72.4 %all-reduce.24.cloned.1.call-done = f32[1,128,256]{2,1,0:T(8,128)} async-done(((f32[1,128,256]{2,1,0:T(8,128)}), f32[1,128,256]{2,1,0:T(8,128)}) %all-reduce.24.cloned.1.call-update) | async-done | bytes 131088 | tf_op jit(solution)/shard_map/psum | solution.py:11
  211.3 111.8 %all-reduce.26.cloned.1.call-done = f32[4,128,256]{2,1,0:T(8,128)} async-done(((f32[4,128,256]{2,1,0:T(8,128)}), f32[4,128,256]{2,1,0:T(8,128)}) %all-reduce.26.cloned.1.call-update) | async-done | bytes 524304 | tf_op jit(solution)/shard_map/psum | solution.py:36
  325.1 72.3 %all-reduce.28.cloned.1.call-done = f32[1,128,256]{2,1,0:T(8,128)} async-done(((f32[1,128,256]{2,1,0:T(8,128)}), f32[1,128,256]{2,1,0:T(8,128)}) %all-reduce.28.cloned.1.call-update) | async-done | bytes 131088 | tf_op jit(solution)/shard_map/psum | solution.py:11
  400.5 111.6 %all-reduce.30.cloned.1.call-done = f32[4,128,256]{2,1,0:T(8,128)} async-done(((f32[4,128,256]{2,1,0:T(8,128)}), f32[4,128,256]{2,1,0:T(8,128)}) %all-reduce.30.cloned.1.call-update) | async-done | bytes 524304 | tf_op jit(solution)/shard_map/psum | solution.py:36
  514.0 72.3 %all-reduce.32.cloned.1.call-done = f32[1,128,256]{2,1,0:T(8,128)} async-done(((f32[1,128,256]{2,1,0:T(8,128)}), f32[1,128,256]{2,1,0:T(8,128)}) %all-reduce.32.cloned.1.call-update) | async-done | bytes 131088 | tf_op jit(solution)/shard_map/psum | solution.py:11
  589.5 111.6 %all-reduce.34.cloned.1.call-done = f32[4,128,256]{2,1,0:T(8,128)} async-done(((f32[4,128,256]{2,1,0:T(8,128)}), f32[4,128,256]{2,1,0:T(8,128)}) %all-reduce.34.cloned.1.call-update) | async-done | bytes 524304 | tf_op jit(solution)/shard_map/psum | solution.py:36
  703.1 72.4 %all-reduce.36.cloned.1.call-done = f32[1,128,256]{2,1,0:T(8,128)} async-done(((f32[1,128,256]{2,1,0:T(8,128)}), f32[1,128,256]{2,1,0:T(8,128)}) %all-reduce.36.cloned.1.call-update) | async-done | bytes 131088 | tf_op jit(solution)/shard_map/psum | solution.py:11
  778.8 111.6 %all-reduce.38.cloned.1.call-done = f32[4,128,256]{2,1,0:T(8,128)} async-done(((f32[4,128,256]{2,1,0:T(8,128)}), f32[4,128,256]{2,1,0:T(8,128)}) %all-reduce.38.cloned.1.call-update) | async-done | bytes 524304 | tf_op jit(solution)/shard_map/psum | solution.py:36
  892.3 72.3 %all-reduce.40.cloned.1.call-done = f32[1,128,256]{2,1,0:T(8,128)} async-done(((f32[1,128,256]{2,1,0:T(8,128)}), f32[1,128,256]{2,1,0:T(8,128)}) %all-reduce.40.cloned.1.call-update) | async-done | bytes 131088 | tf_op jit(solution)/shard_map/psum | solution.py:11
  965.6 2.3 convolution_bitcast_fusion.1
  967.9 111.7 %all-reduce.42.cloned.1.call-done = f32[4,128,256]{2,1,0:T(8,128)} async-done(((f32[4,128,256]{2,1,0:T(8,128)}), f32[4,128,256]{2,1,0:T(8,128)}) %all-reduce.42.cloned.1.call-update) | async-done | bytes 524304 | tf_op jit(solution)/shard_map/psum | solution.py:36
  1081.5 72.3 %all-reduce.44.cloned.1.call-done = f32[1,128,256]{2,1,0:T(8,128)} async-done(((f32[1,128,256]{2,1,0:T(8,128)}), f32[1,128,256]{2,1,0:T(8,128)}) %all-reduce.44.cloned.1.call-update) | async-done | bytes 131088 | tf_op jit(solution)/shard_map/psum | solution.py:11
  1154.8 2.4 convolution_bitcast_fusion
  1157.2 111.7 %all-reduce.46.cloned.1.call-done = f32[4,128,256]{2,1,0:T(8,128)} async-done(((f32[4,128,256]{2,1,0:T(8,128)}), f32[4,128,256]{2,1,0:T(8,128)}) %all-reduce.46.cloned.1.call-update) | async-done | bytes 524304 | tf_op jit(solution)/shard_map/psum | solution.py:36
  1270.8 72.3 %all-reduce.48.cloned.1.call-done = f32[128,256]{1,0:T(8,128)} async-done(((f32[128,256]{1,0:T(8,128)}), f32[128,256]{1,0:T(8,128)}) %all-reduce.48.cloned.1.call-update) | async-done | bytes 131088 | tf_op jit(solution)/shard_map/psum | solution.py:11
  1345.2 48.3 %all-gather.15.cloned.1.call-done = bf16[4096,256]{0,1:T(8,128)(2,1)} async-done(((bf16[128,256]{0,1:T(8,128)(2,1)}), bf16[4096,256]{0,1:T(8,128)(2,1)}) %all-gather.15.cloned.1.call-update) | async-done | bytes 2097168 | tf_op jit(solution)/shard_map/all_gather | solution.py:72
  1398.4 71.8 %all-reduce.50.cloned.1.call-done = f32[1,128,256]{2,1,0:T(8,128)} async-done(((f32[1,128,256]{2,1,0:T(8,128)}), f32[1,128,256]{2,1,0:T(8,128)}) %all-reduce.50.cloned.1.call-update) | async-done | bytes 131088 | tf_op jit(solution)/shard_map/psum | solution.py:67
  1472.2 48.6 %all-gather.17.cloned.1.call-done = bf16[4096,256]{0,1:T(8,128)(2,1)} async-done(((bf16[128,256]{0,1:T(8,128)(2,1)}), bf16[4096,256]{0,1:T(8,128)(2,1)}) %all-gather.17.cloned.1.call-update) | async-done | bytes 2097168 | tf_op jit(solution)/shard_map/all_gather | solution.py:72
  1525.9 71.8 %all-reduce.52.cloned.1.call-done = f32[1,128,256]{2,1,0:T(8,128)} async-done(((f32[1,128,256]{2,1,0:T(8,128)}), f32[1,128,256]{2,1,0:T(8,128)}) %all-reduce.52.cloned.1.call-update) | async-done | bytes 131088 | tf_op jit(solution)/shard_map/psum | solution.py:67
  1599.6 48.4 %all-gather.19.cloned.1.call-done = bf16[4096,256]{0,1:T(8,128)(2,1)} async-done(((bf16[128,256]{0,1:T(8,128)(2,1)}), bf16[4096,256]{0,1:T(8,128)(2,1)}) %all-gather.19.cloned.1.call-update) | async-done | bytes 2097168 | tf_op jit(solution)/shard_map/all_gather | solution.py:72
  1653.2 71.8 %all-reduce.54.cloned.1.call-done = f32[1,128,256]{2,1,0:T(8,128)} async-done(((f32[1,128,256]{2,1,0:T(8,128)}), f32[1,128,256]{2,1,0:T(8,128)}) %all-reduce.54.cloned.1.call-update) | async-done | bytes 131088 | tf_op jit(solution)/shard_map/psum | solution.py:67
  1727.2 48.6 %all-gather.21.cloned.1.call-done = bf16[4096,256]{0,1:T(8,128)(2,1)} async-done(((bf16[128,256]{0,1:T(8,128)(2,1)}), bf16[4096,256]{0,1:T(8,128)(2,1)}) %all-gather.21.cloned.1.call-update) | async-done | bytes 2097168 | tf_op jit(solution)/shard_map/all_gather | solution.py:72
  1781.1 71.8 %all-reduce.56.cloned.1.call-done = f32[1,128,256]{2,1,0:T(8,128)} async-done(((f32[1,128,256]{2,1,0:T(8,128)}), f32[1,128,256]{2,1,0:T(8,128)}) %all-reduce.56.cloned.1.call-update) | async-done | bytes 131088 | tf_op jit(solution)/shard_map/psum | solution.py:67
  1854.9 48.4 %all-gather.23.cloned.1.call-done = bf16[4096,256]{0,1:T(8,128)(2,1)} async-done(((bf16[128,256]{0,1:T(8,128)(2,1)}), bf16[4096,256]{0,1:T(8,128)(2,1)}) %all-gather.23.cloned.1.call-update) | async-done | bytes 2097168 | tf_op jit(solution)/shard_map/all_gather | solution.py:72
  1908.8 71.8 %all-reduce.58.cloned.1.call-done = f32[1,128,256]{2,1,0:T(8,128)} async-done(((f32[1,128,256]{2,1,0:T(8,128)}), f32[1,128,256]{2,1,0:T(8,128)}) %all-reduce.58.cloned.1.call-update) | async-done | bytes 131088 | tf_op jit(solution)/shard_map/psum | solution.py:67
  1982.6 48.7 %all-gather.25.cloned.1.call-done = bf16[4096,256]{0,1:T(8,128)(2,1)} async-done(((bf16[128,256]{0,1:T(8,128)(2,1)}), bf16[4096,256]{0,1:T(8,128)(2,1)}) %all-gather.25.cloned.1.call-update) | async-done | bytes 2097168 | tf_op jit(solution)/shard_map/all_gather | solution.py:72
  2036.8 71.8 %all-reduce.60.cloned.1.call-done = f32[1,128,256]{2,1,0:T(8,128)} async-done(((f32[1,128,256]{2,1,0:T(8,128)}), f32[1,128,256]{2,1,0:T(8,128)}) %all-reduce.60.cloned.1.call-update) | async-done | bytes 131088 | tf_op jit(solution)/shard_map/psum | solution.py:67
  2110.7 48.2 %all-gather.27.cloned.1.call-done = bf16[4096,256]{0,1:T(8,128)(2,1)} async-done(((bf16[128,256]{0,1:T(8,128)(2,1)}), bf16[4096,256]{0,1:T(8,128)(2,1)}) %all-gather.27.cloned.1.call-update) | async-done | bytes 2097168 | tf_op jit(solution)/shard_map/all_gather | solution.py:72
  2162.2 2.4 convolution_bitcast_fusion.6
  2164.6 71.8 %all-reduce.62.cloned.1.call-done = f32[1,128,256]{2,1,0:T(8,128)} async-done(((f32[1,128,256]{2,1,0:T(8,128)}), f32[1,128,256]{2,1,0:T(8,128)}) %all-reduce.62.cloned.1.call-update) | async-done | bytes 131088 | tf_op jit(solution)/shard_map/psum | solution.py:67
  (165 shorter events, 82.8 us)
Async XLA Ops:
  6.5 127.4 %all-reduce.22.cloned.1.call-start = ((), (), s32[]{:S(2)}) async-start(), calls=%async_computation | async-start | bytes 1048576 | tf_op jit(solution)/shard_map/psum | solution.py:36
  8.4 125.5 %copy-start = (f32[8,1,128,128]{3,2,1,0:T(8,128)S(1)}, f32[8,1,128,128]{3,2,1,0:T(8,128)}, u32[]{:S(2)}) copy-start(f32[8,1,128,128]{3,2,1,0:T(8,128)} %param.7) | copy-start | bytes 1572868
  8.5 125.5 %copy-start.1 = (f32[8,1,128,256]{3,2,1,0:T(8,128)S(1)}, f32[8,1,128,256]{3,2,1,0:T(8,128)}, u32[]{:S(2)}) copy-start(f32[8,1,128,256]{3,2,1,0:T(8,128)} %param.6) | copy-start | bytes 3145732
  17.8 190.6 %all-reduce.24.cloned.1.call-start = ((), (), s32[]{:S(2)}) async-start(), calls=%async_computation.1 | async-start | bytes 262144 | tf_op jit(solution)/shard_map/psum | solution.py:11
  135.8 187.3 %all-reduce.26.cloned.1.call-start = ((), (), s32[]{:S(2)}) async-start(), calls=%async_computation.2 | async-start | bytes 1048576 | tf_op jit(solution)/shard_map/psum | solution.py:36
  211.3 186.1 %all-reduce.28.cloned.1.call-start = ((), (), s32[]{:S(2)}) async-start(), calls=%async_computation.3 | async-start | bytes 262144 | tf_op jit(solution)/shard_map/psum | solution.py:11
  325.0 187.1 %all-reduce.30.cloned.1.call-start = ((), (), s32[]{:S(2)}) async-start(), calls=%async_computation.4 | async-start | bytes 1048576 | tf_op jit(solution)/shard_map/psum | solution.py:36
  400.4 185.9 %all-reduce.32.cloned.1.call-start = ((), (), s32[]{:S(2)}) async-start(), calls=%async_computation.5 | async-start | bytes 262144 | tf_op jit(solution)/shard_map/psum | solution.py:11
  514.0 187.1 %all-reduce.34.cloned.1.call-start = ((), (), s32[]{:S(2)}) async-start(), calls=%async_computation.6 | async-start | bytes 1048576 | tf_op jit(solution)/shard_map/psum | solution.py:36
  589.4 186.1 %all-reduce.36.cloned.1.call-start = ((), (), s32[]{:S(2)}) async-start(), calls=%async_computation.7 | async-start | bytes 262144 | tf_op jit(solution)/shard_map/psum | solution.py:11
  703.0 187.4 %all-reduce.38.cloned.1.call-start = ((), (), s32[]{:S(2)}) async-start(), calls=%async_computation.8 | async-start | bytes 1048576 | tf_op jit(solution)/shard_map/psum | solution.py:36
  778.7 185.9 %all-reduce.40.cloned.1.call-start = ((), (), s32[]{:S(2)}) async-start(), calls=%async_computation.9 | async-start | bytes 262144 | tf_op jit(solution)/shard_map/psum | solution.py:11
  892.3 187.3 %all-reduce.42.cloned.1.call-start = ((), (), s32[]{:S(2)}) async-start(), calls=%async_computation.10 | async-start | bytes 1048576 | tf_op jit(solution)/shard_map/psum | solution.py:36
  967.9 186.0 %all-reduce.44.cloned.1.call-start = ((), (), s32[]{:S(2)}) async-start(), calls=%async_computation.11 | async-start | bytes 262144 | tf_op jit(solution)/shard_map/psum | solution.py:11
  1081.5 187.4 %all-reduce.46.cloned.1.call-start = ((), (), s32[]{:S(2)}) async-start(), calls=%async_computation.12 | async-start | bytes 1048576 | tf_op jit(solution)/shard_map/psum | solution.py:36
  1157.2 186.0 %all-reduce.48.cloned.1.call-start = ((), (), s32[]{:S(2)}) async-start(), calls=%async_computation.13 | async-start | bytes 262144 | tf_op jit(solution)/shard_map/psum | solution.py:11
  1270.8 122.7 %all-gather.15.cloned.1.call-start = ((), (), s32[]{:S(2)}) async-start(), calls=%async_computation.21 | async-start | bytes 2162688 | tf_op jit(solution)/shard_map/all_gather | solution.py:72
  1345.1 125.1 %all-reduce.50.cloned.1.call-start = ((), (), s32[]{:S(2)}) async-start(), calls=%async_computation.14 | async-start | bytes 262144 | tf_op jit(solution)/shard_map/psum | solution.py:67
  1398.4 122.4 %all-gather.17.cloned.1.call-start = ((), (), s32[]{:S(2)}) async-start(), calls=%async_computation.22 | async-start | bytes 2162688 | tf_op jit(solution)/shard_map/all_gather | solution.py:72
  1472.1 125.5 %all-reduce.52.cloned.1.call-start = ((), (), s32[]{:S(2)}) async-start(), calls=%async_computation.15 | async-start | bytes 262144 | tf_op jit(solution)/shard_map/psum | solution.py:67
  1525.8 122.3 %all-gather.19.cloned.1.call-start = ((), (), s32[]{:S(2)}) async-start(), calls=%async_computation.23 | async-start | bytes 2162688 | tf_op jit(solution)/shard_map/all_gather | solution.py:72
  1599.6 125.4 %all-reduce.54.cloned.1.call-start = ((), (), s32[]{:S(2)}) async-start(), calls=%async_computation.16 | async-start | bytes 262144 | tf_op jit(solution)/shard_map/psum | solution.py:67
  1653.2 122.6 %all-gather.21.cloned.1.call-start = ((), (), s32[]{:S(2)}) async-start(), calls=%async_computation.24 | async-start | bytes 2162688 | tf_op jit(solution)/shard_map/all_gather | solution.py:72
  1727.0 125.9 %all-reduce.56.cloned.1.call-start = ((), (), s32[]{:S(2)}) async-start(), calls=%async_computation.17 | async-start | bytes 262144 | tf_op jit(solution)/shard_map/psum | solution.py:67
  1781.0 122.3 %all-gather.23.cloned.1.call-start = ((), (), s32[]{:S(2)}) async-start(), calls=%async_computation.25 | async-start | bytes 2162688 | tf_op jit(solution)/shard_map/all_gather | solution.py:72
  1854.8 125.7 %all-reduce.58.cloned.1.call-start = ((), (), s32[]{:S(2)}) async-start(), calls=%async_computation.18 | async-start | bytes 262144 | tf_op jit(solution)/shard_map/psum | solution.py:67
  1908.7 122.6 %all-gather.25.cloned.1.call-start = ((), (), s32[]{:S(2)}) async-start(), calls=%async_computation.26 | async-start | bytes 2162688 | tf_op jit(solution)/shard_map/all_gather | solution.py:72
  1982.5 126.1 %all-reduce.60.cloned.1.call-start = ((), (), s32[]{:S(2)}) async-start(), calls=%async_computation.19 | async-start | bytes 262144 | tf_op jit(solution)/shard_map/psum | solution.py:67
  2036.8 122.1 %all-gather.27.cloned.1.call-start = ((), (), s32[]{:S(2)}) async-start(), calls=%async_computation.27 | async-start | bytes 2162688 | tf_op jit(solution)/shard_map/all_gather | solution.py:72
  2110.6 125.8 %all-reduce.62.cloned.1.call-start = ((), (), s32[]{:S(2)}) async-start(), calls=%async_computation.20 | async-start | bytes 262144 | tf_op jit(solution)/shard_map/psum | solution.py:67
  2162.2 75.6 %copy-start.8 = (f32[256,128]{1,0:T(8,128)S(1)}, f32[256,128]{1,0:T(8,128)}, u32[]{:S(2)}) copy-start(f32[256,128]{1,0:T(8,128)} %get-tuple-element.37) | copy-start | bytes 393220
  2162.2 75.6 %copy-start.7 = (f32[256,128]{1,0:T(8,128)S(1)}, f32[256,128]{1,0:T(8,128)}, u32[]{:S(2)}) copy-start(f32[256,128]{1,0:T(8,128)} %get-tuple-element.35) | copy-start | bytes 393220
  (7 other events, 521.5 us)
Sparse Core Ops, SparseCore 0:
  17.9 116.0 all-reduce.21
  136.4 71.9 all-reduce.23
  211.6 111.5 all-reduce.25
  325.4 71.9 all-reduce.27
  400.5 111.5 all-reduce.29
  514.4 71.9 all-reduce.31
  589.5 111.5 all-reduce.33
  703.5 71.9 all-reduce.35
  778.8 111.5 all-reduce.37
  892.7 71.9 all-reduce.39
  968.0 111.5 all-reduce.41
  1081.9 71.9 all-reduce.43
  1157.3 111.5 all-reduce.45
  1271.2 71.9 all-reduce.47
  1345.5 47.9 all-gather.14
  1398.5 71.6 all-reduce.49
  1472.8 47.9 all-gather.16
  1525.9 71.6 all-reduce.51
  1600.1 47.9 all-gather.18
  1653.3 71.6 all-reduce.53
  1727.8 47.9 all-gather.20
  1781.1 71.6 all-reduce.55
  1855.3 47.9 all-gather.22
  1908.8 71.6 all-reduce.57
  1983.3 47.9 all-gather.24
  2036.9 71.6 all-reduce.59
  2110.9 47.9 all-gather.26
  2164.7 71.6 all-reduce.61
where the time goes:
time: 2250 us
  waiting for transfers between devices  2130 us (95%)
  matrix products  58.4 us (3%)
  local copies, waits for them, and re-layouts  23.5 us (1%)
    psum x7, waiting for transfers between devices, per_device(): row_total = lax.psum(partial_sum, 'col')  786 us
    psum x7, waiting for transfers between devices, spread(): return lax.psum(kept, axis)  507 us
    psum x7, waiting for transfers between devices, per_device(): resid = resid - lax.psum(partial_sum, 'row')  502 us
    all_gather x7, waiting for transfers between devices, per_device(): pieces = lax.all_gather(low_solved[None], 'col', axis=0, tiled=True)  339 us
  transfers between devices with their start and end apart: 28, of which 28 were waited for; matrix products, arithmetic and copies ran while one was open for 0% of the time, Pallas kernels for 0%

commit v1 on v0

--- a/solution.py
+++ b/solution.py
@@ -69,7 +69,10 @@
         solution_parts[level_id] = solved
         if level_id > 0:
             low_solved = solved.astype(jnp.bfloat16)
-            pieces = lax.all_gather(low_solved[None], "col", axis=0, tiled=True)
+            pieces = jnp.concatenate(
+                lax.all_to_all(jnp.stack([low_solved[None]] * lax.axis_size("col")), "col", 0, 0),
+                axis=0,
+            )
             pieces = pieces.reshape((groups, row_count) + low_solved.shape)
             picked = lax.dynamic_index_in_dim(pieces, my_row, axis=1, keepdims=False)
             arranged = jnp.swapaxes(picked, 0, 1).reshape((per_row,) + low_solved.shape[1:])

time: 2250 us -> 2130 us (0.947)
  waiting for transfers between devices: 2130 us -> 1800 us
  blocking collectives: 0 us -> 208 us
    all_gather x7 -> x0, waiting for transfers between devices: 339 us -> none  [per_device(): pieces = lax.all_gather(low_solved[None], 'col', axis=0, tiled=True)]
    all_to_all x0 -> x6, blocking collectives: none -> 208 us  [per_device(): lax.all_to_all(jnp.stack([low_solved[None]] * lax.axis_size('col')), 'col...]
    all_to_all x0 -> x1, waiting for transfers between devices: none -> 27.8 us  [per_device(): lax.all_to_all(jnp.stack([low_solved[None]] * lax.axis_size('col')), 'col...]
    psum x7, waiting for transfers between devices: 502 us -> 475 us  [per_device(): resid = resid - lax.psum(partial_sum, 'row')]
  transfers between devices with their start and end apart: 28 -> 22, of which waited for: 28 -> 22; matrix products, arithmetic and copies ran while one was open for 0% -> 0% of each run, Pallas kernels for 0% -> 0%
where the time goes in v1:
time: 2130 us; the launch traced here: 2120 us
  waiting for transfers between devices  1800 us (85%)
  blocking collectives  208 us (10%)
  matrix products  56.6 us (3%)
  local copies, waits for them, and re-layouts  27 us (1%)
    psum x7, waiting for transfers between devices, per_device(): row_total = lax.psum(partial_sum, 'col')  786 us
    psum x7, waiting for transfers between devices, spread(): return lax.psum(kept, axis)  507 us
    psum x7, waiting for transfers between devices, per_device(): resid = resid - lax.psum(partial_sum, 'row')  475 us
    all_to_all x6, blocking collectives, per_device(): lax.all_to_all(jnp.stack([low_solved[None]] * lax.axis_size('col')), 'col...  208 us
  transfers between devices with their start and end apart: 22, of which 22 were waited for; matrix products, arithmetic and copies ran while one was open for 0% of the time, Pallas kernels for 0%

profile of v1, /device:TPU:2, one launch (start us, length us, event | category | flops | bytes accessed | tf_op | source)
XLA Modules:
  0.0 2124.0 jit_solution(9156986208300780044)
XLA Ops:
  8.5 7.4 bitcast_multiply_fusion
  17.9 116.1 %all-reduce.22.cloned.1.call-done = f32[4,128,256]{2,1,0:T(8,128)} async-done(((f32[4,128,256]{2,1,0:T(8,128)}), f32[4,128,256]{2,1,0:T(8,128)}) %all-reduce.22.cloned.1.call-update) | async-done | bytes 524304 | tf_op jit(solution)/shard_map/psum | solution.py:36
  135.9 72.5 %all-reduce.24.cloned.1.call-done = f32[1,128,256]{2,1,0:T(8,128)} async-done(((f32[1,128,256]{2,1,0:T(8,128)}), f32[1,128,256]{2,1,0:T(8,128)}) %all-reduce.24.cloned.1.call-update) | async-done | bytes 131088 | tf_op jit(solution)/shard_map/psum | solution.py:11
  211.3 111.8 %all-reduce.26.cloned.1.call-done = f32[4,128,256]{2,1,0:T(8,128)} async-done(((f32[4,128,256]{2,1,0:T(8,128)}), f32[4,128,256]{2,1,0:T(8,128)}) %all-reduce.26.cloned.1.call-update) | async-done | bytes 524304 | tf_op jit(solution)/shard_map/psum | solution.py:36
  325.0 72.3 %all-reduce.28.cloned.1.call-done = f32[1,128,256]{2,1,0:T(8,128)} async-done(((f32[1,128,256]{2,1,0:T(8,128)}), f32[1,128,256]{2,1,0:T(8,128)}) %all-reduce.28.cloned.1.call-update) | async-done | bytes 131088 | tf_op jit(solution)/shard_map/psum | solution.py:11
  400.5 111.7 %all-reduce.30.cloned.1.call-done = f32[4,128,256]{2,1,0:T(8,128)} async-done(((f32[4,128,256]{2,1,0:T(8,128)}), f32[4,128,256]{2,1,0:T(8,128)}) %all-reduce.30.cloned.1.call-update) | async-done | bytes 524304 | tf_op jit(solution)/shard_map/psum | solution.py:36
  514.0 72.3 %all-reduce.32.cloned.1.call-done = f32[1,128,256]{2,1,0:T(8,128)} async-done(((f32[1,128,256]{2,1,0:T(8,128)}), f32[1,128,256]{2,1,0:T(8,128)}) %all-reduce.32.cloned.1.call-update) | async-done | bytes 131088 | tf_op jit(solution)/shard_map/psum | solution.py:11
  589.5 111.6 %all-reduce.34.cloned.1.call-done = f32[4,128,256]{2,1,0:T(8,128)} async-done(((f32[4,128,256]{2,1,0:T(8,128)}), f32[4,128,256]{2,1,0:T(8,128)}) %all-reduce.34.cloned.1.call-update) | async-done | bytes 524304 | tf_op jit(solution)/shard_map/psum | solution.py:36
  703.1 72.4 %all-reduce.36.cloned.1.call-done = f32[1,128,256]{2,1,0:T(8,128)} async-done(((f32[1,128,256]{2,1,0:T(8,128)}), f32[1,128,256]{2,1,0:T(8,128)}) %all-reduce.36.cloned.1.call-update) | async-done | bytes 131088 | tf_op jit(solution)/shard_map/psum | solution.py:11
  778.8 111.7 %all-reduce.38.cloned.1.call-done = f32[4,128,256]{2,1,0:T(8,128)} async-done(((f32[4,128,256]{2,1,0:T(8,128)}), f32[4,128,256]{2,1,0:T(8,128)}) %all-reduce.38.cloned.1.call-update) | async-done | bytes 524304 | tf_op jit(solution)/shard_map/psum | solution.py:36
  892.3 72.3 %all-reduce.40.cloned.1.call-done = f32[1,128,256]{2,1,0:T(8,128)} async-done(((f32[1,128,256]{2,1,0:T(8,128)}), f32[1,128,256]{2,1,0:T(8,128)}) %all-reduce.40.cloned.1.call-update) | async-done | bytes 131088 | tf_op jit(solution)/shard_map/psum | solution.py:11
  968.0 111.7 %all-reduce.42.cloned.1.call-done = f32[4,128,256]{2,1,0:T(8,128)} async-done(((f32[4,128,256]{2,1,0:T(8,128)}), f32[4,128,256]{2,1,0:T(8,128)}) %all-reduce.42.cloned.1.call-update) | async-done | bytes 524304 | tf_op jit(solution)/shard_map/psum | solution.py:36
  1081.5 72.3 %all-reduce.44.cloned.1.call-done = f32[1,128,256]{2,1,0:T(8,128)} async-done(((f32[1,128,256]{2,1,0:T(8,128)}), f32[1,128,256]{2,1,0:T(8,128)}) %all-reduce.44.cloned.1.call-update) | async-done | bytes 131088 | tf_op jit(solution)/shard_map/psum | solution.py:11
  1154.8 2.4 convolution_bitcast_fusion
  1157.3 111.6 %all-reduce.46.cloned.1.call-done = f32[4,128,256]{2,1,0:T(8,128)} async-done(((f32[4,128,256]{2,1,0:T(8,128)}), f32[4,128,256]{2,1,0:T(8,128)}) %all-reduce.46.cloned.1.call-update) | async-done | bytes 524304 | tf_op jit(solution)/shard_map/psum | solution.py:36
  1270.8 72.4 %all-reduce.48.cloned.1.call-done = f32[128,256]{1,0:T(8,128)} async-done(((f32[128,256]{1,0:T(8,128)}), f32[128,256]{1,0:T(8,128)}) %all-reduce.48.cloned.1.call-update) | async-done | bytes 131088 | tf_op jit(solution)/shard_map/psum | solution.py:11
  1346.2 7.5 all-to-all-start
  1353.8 27.8 %all-to-all-done = bf16[32,1,1,128,256]{4,3,2,1,0:T(8,128)(2,1)S(1)} async-done(((bf16[32,1,1,128,256]{4,3,2,1,0:T(8,128)(2,1)}), bf16[32,1,1,128,256]{4,3,2,1,0:T(8,128)(2,1)S(1)}, u32[]{:S(2)}, u32[]{:S(2)}) %all-to-all-start) | async-done | bytes 2097184 | tf_op jit(solution)/shard_map/all_to_all | solution.py:73
  1383.5 68.2 %all-reduce.50.cloned.1.call-done = f32[1,128,256]{2,1,0:T(8,128)} async-done(((f32[1,128,256]{2,1,0:T(8,128)}), f32[1,128,256]{2,1,0:T(8,128)}) %all-reduce.50.cloned.1.call-update) | async-done | bytes 131088 | tf_op jit(solution)/shard_map/psum | solution.py:67
  1453.4 34.7 %all_to_all.35 = bf16[32,1,1,128,256]{4,3,2,1,0:T(8,128)(2,1)S(1)} all-to-all(bf16[32,1,1,128,256]{4,3,2,1,0:T(8,128)(2,1)S(1)} %stack.22), channel_id=1, replica_groups=mesh['row'=8,'col'=32] {'col'}, dimensions={0} | all-to-all | bytes 4194304 | tf_op jit(solution)/shard_map/all_to_all | solution.py:73
  1492.1 67.9 %all-reduce.52.cloned.1.call-done = f32[1,128,256]{2,1,0:T(8,128)} async-done(((f32[1,128,256]{2,1,0:T(8,128)}), f32[1,128,256]{2,1,0:T(8,128)}) %all-reduce.52.cloned.1.call-update) | async-done | bytes 131088 | tf_op jit(solution)/shard_map/psum | solution.py:67
  1563.1 34.7 %all_to_all.36 = bf16[32,1,1,128,256]{4,3,2,1,0:T(8,128)(2,1)S(1)} all-to-all(bf16[32,1,1,128,256]{4,3,2,1,0:T(8,128)(2,1)S(1)} %stack.23), channel_id=1, replica_groups=mesh['row'=8,'col'=32] {'col'}, dimensions={0} | all-to-all | bytes 4194304 | tf_op jit(solution)/shard_map/all_to_all | solution.py:73
  1601.9 67.9 %all-reduce.54.cloned.1.call-done = f32[1,128,256]{2,1,0:T(8,128)} async-done(((f32[1,128,256]{2,1,0:T(8,128)}), f32[1,128,256]{2,1,0:T(8,128)}) %all-reduce.54.cloned.1.call-update) | async-done | bytes 131088 | tf_op jit(solution)/shard_map/psum | solution.py:67
  1673.0 34.7 %all_to_all.37 = bf16[32,1,1,128,256]{4,3,2,1,0:T(8,128)(2,1)S(1)} all-to-all(bf16[32,1,1,128,256]{4,3,2,1,0:T(8,128)(2,1)S(1)} %stack.24), channel_id=1, replica_groups=mesh['row'=8,'col'=32] {'col'}, dimensions={0} | all-to-all | bytes 4194304 | tf_op jit(solution)/shard_map/all_to_all | solution.py:73
  1711.3 67.9 %all-reduce.56.cloned.1.call-done = f32[1,128,256]{2,1,0:T(8,128)} async-done(((f32[1,128,256]{2,1,0:T(8,128)}), f32[1,128,256]{2,1,0:T(8,128)}) %all-reduce.56.cloned.1.call-update) | async-done | bytes 131088 | tf_op jit(solution)/shard_map/psum | solution.py:67
  1780.8 34.6 %all_to_all.38 = bf16[32,1,1,128,256]{4,3,2,1,0:T(8,128)(2,1)S(1)} all-to-all(bf16[32,1,1,128,256]{4,3,2,1,0:T(8,128)(2,1)S(1)} %stack.25), channel_id=1, replica_groups=mesh['row'=8,'col'=32] {'col'}, dimensions={0} | all-to-all | bytes 4194304 | tf_op jit(solution)/shard_map/all_to_all | solution.py:73
  1822.1 67.7 %all-reduce.58.cloned.1.call-done = f32[1,128,256]{2,1,0:T(8,128)} async-done(((f32[1,128,256]{2,1,0:T(8,128)}), f32[1,128,256]{2,1,0:T(8,128)}) %all-reduce.58.cloned.1.call-update) | async-done | bytes 131088 | tf_op jit(solution)/shard_map/psum | solution.py:67
  1892.1 34.6 %all_to_all.39 = bf16[32,1,1,128,256]{4,3,2,1,0:T(8,128)(2,1)S(1)} all-to-all(bf16[32,1,1,128,256]{4,3,2,1,0:T(8,128)(2,1)S(1)} %stack.26), channel_id=1, replica_groups=mesh['row'=8,'col'=32] {'col'}, dimensions={0} | all-to-all | bytes 4194304 | tf_op jit(solution)/shard_map/all_to_all | solution.py:73
  1934.4 67.9 %all-reduce.60.cloned.1.call-done = f32[1,128,256]{2,1,0:T(8,128)} async-done(((f32[1,128,256]{2,1,0:T(8,128)}), f32[1,128,256]{2,1,0:T(8,128)}) %all-reduce.60.cloned.1.call-update) | async-done | bytes 131088 | tf_op jit(solution)/shard_map/psum | solution.py:67
  2004.5 34.6 %all_to_all.40 = bf16[32,1,1,128,256]{4,3,2,1,0:T(8,128)(2,1)S(1)} all-to-all(bf16[32,1,1,128,256]{4,3,2,1,0:T(8,128)(2,1)S(1)} %stack.27), channel_id=1, replica_groups=mesh['row'=8,'col'=32] {'col'}, dimensions={0} | all-to-all | bytes 4194304 | tf_op jit(solution)/shard_map/all_to_all | solution.py:73
  2044.1 2.4 convolution_bitcast_fusion.6
  2046.5 67.9 %all-reduce.62.cloned.1.call-done = f32[1,128,256]{2,1,0:T(8,128)} async-done(((f32[1,128,256]{2,1,0:T(8,128)}), f32[1,128,256]{2,1,0:T(8,128)}) %all-reduce.62.cloned.1.call-update) | async-done | bytes 131088 | tf_op jit(solution)/shard_map/psum | solution.py:67
  (169 shorter events, 86.4 us)
Async XLA Ops:
  6.5 127.4 %all-reduce.22.cloned.1.call-start = ((), (), s32[]{:S(2)}) async-start(), calls=%async_computation.7 | async-start | bytes 1048576 | tf_op jit(solution)/shard_map/psum | solution.py:36
  8.4 125.5 %copy-start.5 = (f32[8,1,128,128]{3,2,1,0:T(8,128)S(1)}, f32[8,1,128,128]{3,2,1,0:T(8,128)}, u32[]{:S(2)}) copy-start(f32[8,1,128,128]{3,2,1,0:T(8,128)} %param.7) | copy-start | bytes 1572868
  8.5 125.5 %copy-start.6 = (f32[8,1,128,256]{3,2,1,0:T(8,128)S(1)}, f32[8,1,128,256]{3,2,1,0:T(8,128)}, u32[]{:S(2)}) copy-start(f32[8,1,128,256]{3,2,1,0:T(8,128)} %param.6) | copy-start | bytes 3145732
  17.8 190.6 %all-reduce.24.cloned.1.call-start = ((), (), s32[]{:S(2)}) async-start(), calls=%async_computation.8 | async-start | bytes 262144 | tf_op jit(solution)/shard_map/psum | solution.py:11
  135.8 187.3 %all-reduce.26.cloned.1.call-start = ((), (), s32[]{:S(2)}) async-start(), calls=%async_computation.9 | async-start | bytes 1048576 | tf_op jit(solution)/shard_map/psum | solution.py:36
  211.3 186.1 %all-reduce.28.cloned.1.call-start = ((), (), s32[]{:S(2)}) async-start(), calls=%async_computation.10 | async-start | bytes 262144 | tf_op jit(solution)/shard_map/psum | solution.py:11
  325.0 187.1 %all-reduce.30.cloned.1.call-start = ((), (), s32[]{:S(2)}) async-start(), calls=%async_computation.11 | async-start | bytes 1048576 | tf_op jit(solution)/shard_map/psum | solution.py:36
  400.4 186.0 %all-reduce.32.cloned.1.call-start = ((), (), s32[]{:S(2)}) async-start(), calls=%async_computation.12 | async-start | bytes 262144 | tf_op jit(solution)/shard_map/psum | solution.py:11
  514.0 187.1 %all-reduce.34.cloned.1.call-start = ((), (), s32[]{:S(2)}) async-start(), calls=%async_computation.13 | async-start | bytes 1048576 | tf_op jit(solution)/shard_map/psum | solution.py:36
  589.5 186.0 %all-reduce.36.cloned.1.call-start = ((), (), s32[]{:S(2)}) async-start(), calls=%async_computation.14 | async-start | bytes 262144 | tf_op jit(solution)/shard_map/psum | solution.py:11
  703.0 187.4 %all-reduce.38.cloned.1.call-start = ((), (), s32[]{:S(2)}) async-start(), calls=%async_computation.15 | async-start | bytes 1048576 | tf_op jit(solution)/shard_map/psum | solution.py:36
  778.7 186.0 %all-reduce.40.cloned.1.call-start = ((), (), s32[]{:S(2)}) async-start(), calls=%async_computation.16 | async-start | bytes 262144 | tf_op jit(solution)/shard_map/psum | solution.py:11
  892.3 187.3 %all-reduce.42.cloned.1.call-start = ((), (), s32[]{:S(2)}) async-start(), calls=%async_computation.17 | async-start | bytes 1048576 | tf_op jit(solution)/shard_map/psum | solution.py:36
  967.9 186.0 %all-reduce.44.cloned.1.call-start = ((), (), s32[]{:S(2)}) async-start(), calls=%async_computation.18 | async-start | bytes 262144 | tf_op jit(solution)/shard_map/psum | solution.py:11
  1081.5 187.4 %all-reduce.46.cloned.1.call-start = ((), (), s32[]{:S(2)}) async-start(), calls=%async_computation.19 | async-start | bytes 1048576 | tf_op jit(solution)/shard_map/psum | solution.py:36
  1157.2 185.9 %all-reduce.48.cloned.1.call-start = ((), (), s32[]{:S(2)}) async-start(), calls=%async_computation.20 | async-start | bytes 262144 | tf_op jit(solution)/shard_map/psum | solution.py:11
  1346.2 105.6 %copy-start.13 = (f32[1,128,256]{2,1,0:T(8,128)S(1)}, f32[1,128,256]{2,1,0:T(8,128)}, u32[]{:S(2)}) copy-start(f32[1,128,256]{2,1,0:T(8,128)} %all-reduce.44.cloned.1.call-done) | copy-start | bytes 393220
  1346.2 35.4 %all-to-all-start = ((bf16[32,1,1,128,256]{4,3,2,1,0:T(8,128)(2,1)}), bf16[32,1,1,128,256]{4,3,2,1,0:T(8,128)(2,1)S(1)}, u32[]{:S(2)}, u32[]{:S(2)}) async-start(bf16[32,1,1,128,256]{4,3,2,1,0:T(8,128)(2,1)} %stack.21), calls=%async_computation | async-start | bytes 4194304 | tf_op jit(solution)/shard_map/all_to_all | solution.py:73
  1353.7 98.0 %all-reduce.50.cloned.1.call-start = ((), (), s32[]{:S(2)}) async-start(), calls=%async_computation.21 | async-start | bytes 262144 | tf_op jit(solution)/shard_map/psum | solution.py:67
  1383.4 176.5 %all-reduce.52.cloned.1.call-start = ((), (), s32[]{:S(2)}) async-start(), calls=%async_computation.22 | async-start | bytes 262144 | tf_op jit(solution)/shard_map/psum | solution.py:67
  1453.4 106.6 %copy-start.12 = (f32[1,128,256]{2,1,0:T(8,128)S(1)}, f32[1,128,256]{2,1,0:T(8,128)}, u32[]{:S(2)}) copy-start(f32[1,128,256]{2,1,0:T(8,128)} %all-reduce.40.cloned.1.call-done) | copy-start | bytes 393220
  1492.1 177.8 %all-reduce.54.cloned.1.call-start = ((), (), s32[]{:S(2)}) async-start(), calls=%async_computation.23 | async-start | bytes 262144 | tf_op jit(solution)/shard_map/psum | solution.py:67
  1597.8 72.0 %copy-start.10 = (f32[1,128,256]{2,1,0:T(8,128)S(1)}, f32[1,128,256]{2,1,0:T(8,128)}, u32[]{:S(2)}) copy-start(f32[1,128,256]{2,1,0:T(8,128)} %all-reduce.36.cloned.1.call-done) | copy-start | bytes 393220
  1601.9 177.2 %all-reduce.56.cloned.1.call-start = ((), (), s32[]{:S(2)}) async-start(), calls=%async_computation.24 | async-start | bytes 262144 | tf_op jit(solution)/shard_map/psum | solution.py:67
  1711.2 178.6 %all-reduce.58.cloned.1.call-start = ((), (), s32[]{:S(2)}) async-start(), calls=%async_computation.25 | async-start | bytes 262144 | tf_op jit(solution)/shard_map/psum | solution.py:67
  1816.7 73.1 %copy-start.8 = (f32[1,128,256]{2,1,0:T(8,128)S(1)}, f32[1,128,256]{2,1,0:T(8,128)}, u32[]{:S(2)}) copy-start(f32[1,128,256]{2,1,0:T(8,128)} %all-reduce.28.cloned.1.call-done) | copy-start | bytes 393220
  1821.9 180.3 %all-reduce.60.cloned.1.call-start = ((), (), s32[]{:S(2)}) async-start(), calls=%async_computation.26 | async-start | bytes 262144 | tf_op jit(solution)/shard_map/psum | solution.py:67
  1930.0 72.2 %copy-start.7 = (f32[1,128,256]{2,1,0:T(8,128)S(1)}, f32[1,128,256]{2,1,0:T(8,128)}, u32[]{:S(2)}) copy-start(f32[1,128,256]{2,1,0:T(8,128)} %all-reduce.24.cloned.1.call-done) | copy-start | bytes 393220
  1934.3 180.1 %all-reduce.62.cloned.1.call-start = ((), (), s32[]{:S(2)}) async-start(), calls=%async_computation.27 | async-start | bytes 262144 | tf_op jit(solution)/shard_map/psum | solution.py:67
  2044.0 71.7 %copy-start.14 = (f32[256,128]{1,0:T(8,128)S(1)}, f32[256,128]{1,0:T(8,128)}, u32[]{:S(2)}) copy-start(f32[256,128]{1,0:T(8,128)} %get-tuple-element.37) | copy-start | bytes 393220
  2044.1 71.7 %copy-start.15 = (f32[256,128]{1,0:T(8,128)S(1)}, f32[256,128]{1,0:T(8,128)}, u32[]{:S(2)}) copy-start(f32[256,128]{1,0:T(8,128)} %get-tuple-element.39) | copy-start | bytes 393220
  2044.1 71.7 %copy-start.11 = (f32[256,128]{1,0:T(8,128)S(1)}, f32[256,128]{1,0:T(8,128)}, u32[]{:S(2)}) copy-start(f32[256,128]{1,0:T(8,128)} %get-tuple-element.33) | copy-start | bytes 393220
  (11 other events, 187.2 us)
Sparse Core Ops, SparseCore 0:
  17.9 116.0 all-reduce.21
  136.4 71.9 all-reduce.23
  211.5 111.5 all-reduce.25
  325.4 71.9 all-reduce.27
  400.5 111.5 all-reduce.29
  514.4 71.9 all-reduce.31
  589.6 111.4 all-reduce.33
  703.5 71.9 all-reduce.35
  778.8 111.5 all-reduce.37
  892.7 71.9 all-reduce.39
  968.0 111.5 all-reduce.41
  1081.9 71.9 all-reduce.43
  1157.3 111.5 all-reduce.45
  1271.2 71.9 all-reduce.47
  1383.6 68.1 all-reduce.49
  1492.2 67.7 all-reduce.51
  1602.0 67.7 all-reduce.53
  1711.3 67.7 all-reduce.55
  1822.0 67.7 all-reduce.57
  1934.4 67.7 all-reduce.59
  2046.6 67.7 all-reduce.61
